TPU v7x, 128 devices: a whole 4x4x4 slice. The times are simulated.
128 devices in a mesh: row: 4 (over y), col: 8 (over z, core), depth: 4 (over x).
Axes of the slice: x: 4, y: 4, z: 4, core: 2. Of those that a mesh axis runs over, the one named last changes fastest.
Arguments:
- panels: float32 [2, 8192, 512], P(None, ('row', 'depth'), 'col'), may hold values from -6 to 6
- slab: float32 [8192, 4096], P(('row', 'depth'), 'col'), may hold values from -6 to 6
- pivot_one: int32 [512], replicated, may hold values from 512 to 8191, as said below
- pivot_two: int32 [512], replicated, may hold values from 1024 to 8191, as said below
- lower_inv: float32 [2, 512, 512], replicated, may hold values from -1 to 1, as said below
- upper_inv: float32 [2, 512, 512], replicated, may hold values from -1 to 1, as said below
Outputs:
- panels_out: float32 [2, 8192, 512], P(None, ('row', 'depth'), 'col')
- slab_out: float32 [8192, 4096], P(('row', 'depth'), 'col')
Inputs may be any that keep to these rules, and one draw needn't show every extreme that they name: `pivot_one`: 512 distinct rows, none among the first 512. `pivot_two`: 512 distinct rows, none among the first 1024. `lower_inv`: each of the two blocks is lower triangular with ones on its diagonal. `upper_inv`: each of the two blocks is upper triangular with a positive diagonal.
All inputs are finite; a program needn't handle non-finite values.
Results may differ from a plain program's by a relative error of at most 0.000075.
Values sent between devices are 32-bit elements; how exact they have to be, the bound alone decides.
No kernel may reach another device: no remote copies, remote signals or barrier semaphores. Data moves between devices by JAX's collectives and lax.ppermute only.
A program may use at most 128 MiB of HBM per device.

v0:
```python
import jax
import jax.numpy as jnp
from jax import lax
from jax.experimental import pallas as pl
from jax.experimental.pallas import tpu as pltpu
from jax.sharding import PartitionSpec as P


NB = 512
CAP = 96
PEERS = 16
SLOTS = PEERS * CAP
SOME = 64
FEW = PEERS * SOME
HALF = (NB + 2 * CAP) // 2
RD = ("row", "depth")
F32 = jnp.float32
BF16 = jnp.bfloat16
GRANT = 24 * 2**20
VMEM = pl.BlockSpec(memory_space=pltpu.VMEM)
ANY = pl.BlockSpec(memory_space=pl.ANY)
SMEM = pl.BlockSpec(memory_space=pltpu.SMEM)


def iota(shape, axis):
    return lax.broadcasted_iota(jnp.int32, shape, axis)


def split2(x):
    high = x.astype(BF16)
    return high, (x - high.astype(F32)).astype(BF16)


def mm(a, b):
    return jnp.dot(a, b, preferred_element_type=F32)


def dot3(a, b):
    both = jnp.concatenate([a[0], a[1]], axis=1)
    return mm(both, jnp.concatenate([b[0], b[0]], axis=0)) + mm(a[0], b[1])


def cut(parts, rows, cols):
    return tuple(p[rows, cols] for p in parts)


FIRST, LAST, ALL = slice(0, NB // 2), slice(NB // 2, NB), slice(None)


def dot3_upper(a, b):
    left = dot3(cut(a, ALL, FIRST), cut(b, FIRST, FIRST))
    return jnp.concatenate([left, dot3(a, cut(b, ALL, LAST))], axis=1)


def dot3_lower(a, b):
    top = dot3(cut(a, FIRST, FIRST), cut(b, FIRST, ALL))
    return jnp.concatenate([top, dot3(cut(a, LAST, ALL), b)], axis=0)


def pick(onehot, parts):
    width = parts[0].shape[1]
    if width > 128:
        return mm(onehot, parts[0]) + mm(onehot, parts[1])
    both = mm(onehot, jnp.concatenate(parts, axis=1))
    return both[:, :width] + both[:, width:]


def pick_t(onehot, parts):
    both = jnp.concatenate(parts, axis=0)
    both = lax.dot_general(onehot, both, (((1,), (1,)), ((), ())), preferred_element_type=F32)
    return both[:, :128] + both[:, 128:]


def in_first(code):
    return jnp.where((code & 4095) < CAP, (code >> 12) * CAP + (code & 4095), -1)


def column(row):
    return jnp.transpose(jnp.broadcast_to(row, (8, row.shape[1])))[:, :1]


def running(x):
    n = x.shape[1]
    upto = jnp.where(iota((n, n), 0) <= iota((n, n), 1), 1.0, 0.0).astype(BF16)
    return mm(x.astype(BF16), upto)


def down(mask, value):
    return jnp.sum(jnp.where(mask, value, 0.0), axis=0, keepdims=True)


def blocks_onehot(rank, code, first, count):
    k = iota((CAP, NB), 0)
    held = k == rank
    code = in_first(code)
    blocks = [
        jnp.where(held | ((k + (first + b) * CAP) == code), 1.0, 0.0).astype(BF16) for b in range(count)
    ]
    return jnp.concatenate(blocks, axis=0)


def plan_kernel(where_ref, one_ref, two_ref, panel_ref, codes_ref, every_ref, most_ref, out_ref):
    me = where_ref[0]
    one, two = one_ref[...].astype(F32), two_ref[...].astype(F32)
    one_c, two_c = column(one), column(two)
    lane = iota((1, NB), 1).astype(F32)
    sub = iota((NB, 1), 0).astype(F32)
    hit = down(one_c == two, sub + 1.0)
    source = jnp.concatenate([one, jnp.where(hit > 0, hit - 1.0, two)], axis=1)
    again = down(two_c == one, 1.0) > 0
    taken = down(one_c == lane + NB, 1.0) > 0
    onward = down(sub + NB == one, two_c)
    leaves = (
        jnp.where(again, -1.0, jnp.where(one < 2 * NB, onward, one)),
        jnp.where(taken, -1.0, two),
    )
    owner = source.astype(jnp.int32) >> 9
    peer = iota((PEERS, NB), 0)
    takers = [v.astype(jnp.int32) >> 9 for v in leaves]
    parties = [owner[:, :NB], owner[:, NB:], *takers]
    shown = jnp.concatenate([jnp.where(peer == p, 1.0, 0.0) for p in parties], axis=0)
    count = running(shown)
    ranks = shown * (count - 1.0)
    rank_one, rank_two, *taker_rank = [
        jnp.sum(ranks[n * PEERS:(n + 1) * PEERS], axis=0, keepdims=True) for n in range(4)
    ]
    number_one, number_two, *number = [count[n * PEERS:(n + 1) * PEERS, NB - 1:] for n in range(4)]
    in_one = jnp.minimum(number_one, float(SOME))
    longest = [jnp.max(v, axis=0, keepdims=True) for v in number]
    peer = iota((PEERS, 1), 0)
    start_two = in_one + jnp.where(peer == 0, longest[0], jnp.where(peer == 1, longest[1], 0.0))
    start_two = jnp.maximum(start_two, jnp.maximum(CAP - number_two, float(CAP - SOME)))
    place_two = rank_two + jnp.sum(shown[PEERS:2 * PEERS] * start_two, axis=0, keepdims=True)
    place_one = jnp.where(rank_one < SOME, rank_one, rank_one + 2048.0)
    rank = jnp.concatenate([place_one, place_two], axis=1)
    most = jnp.max(rank)
    out_codes, in_codes = [], []
    for q in range(2):
        place = taker_rank[q] + in_one[q:q + 1]
        place = place.astype(jnp.int32)
        most = jnp.maximum(most, jnp.max(jnp.where(takers[q] < 0, 0, place).astype(F32)))
        out_codes.append(jnp.where(takers[q] >= 0, takers[q] * 4096 + place, -1))
        in_codes.append((place + (q * 4096 + 1)).astype(F32))
    most_ref[0] = most.astype(jnp.int32)
    mine = lane + (me * NB).astype(F32)
    out_rank = (down(column(source) == mine, column(rank) + 1.0) - 1.0).astype(jnp.int32)
    out_code = jnp.where(me == 0, out_codes[0], jnp.where(me == 1, out_codes[1], -1))
    hit = column(jnp.concatenate(leaves, axis=1)) == mine
    in_code = down(hit, column(jnp.concatenate(in_codes, axis=1))).astype(jnp.int32) - 1
    codes_ref[0:1] = out_rank
    codes_ref[1:2] = out_code
    codes_ref[2:8] = jnp.zeros((6, NB), jnp.int32)
    every_ref[:, :2 * NB] = owner * 4096 + rank.astype(jnp.int32)
    every_ref[:, 2 * NB:] = in_code
    parts = split2(panel_ref[...])
    for c in range(4):
        onehot = blocks_onehot(out_rank, out_code, 4 * c, 4)
        out_ref[4 * c * CAP:4 * (c + 1) * CAP] = pick_t(onehot, parts)


def make_plan(where, pivot_one, pivot_two, panel_t):
    return pl.pallas_call(
        plan_kernel,
        in_specs=[SMEM] + [VMEM] * 3,
        out_specs=[VMEM, VMEM, SMEM, VMEM],
        out_shape=[
            jax.ShapeDtypeStruct((8, NB), jnp.int32),
            jax.ShapeDtypeStruct((1, 3 * NB), jnp.int32),
            jax.ShapeDtypeStruct((1,), jnp.int32),
            jax.ShapeDtypeStruct((SLOTS, 128), F32),
        ],
        name="make_plan",
    )(where, pivot_one.reshape(1, NB), pivot_two.reshape(1, NB), panel_t)


def pack_kernel(codes_ref, rows_ref, out_ref, parts_ref):
    step = pl.program_id(0)

    @pl.when(step == 0)
    def _():
        for n, part in enumerate(split2(rows_ref[...])):
            parts_ref[n] = part

    onehot = blocks_onehot(codes_ref[0:1], codes_ref[1:2], step * 4, 4)
    out_ref[...] = pick(onehot, (parts_ref[0], parts_ref[1], parts_ref[2]))


def pack(codes, rows):
    width = rows.shape[1]
    return pl.pallas_call(
        pack_kernel,
        grid=(4,),
        in_specs=[pl.BlockSpec((8, NB), lambda i: (0, 0)), pl.BlockSpec((NB, width), lambda i: (0, 0))],
        out_specs=pl.BlockSpec((4 * CAP, width), lambda i: (i, 0)),
        out_shape=jax.ShapeDtypeStruct((SLOTS, width), F32),
        scratch_shapes=[pltpu.VMEM((3, NB, width), BF16)],
        name="pack_rows",
    )(codes, rows)


def slots_of(at_ref, n):
    code = at_ref[:, n * NB:(n + 1) * NB]
    place = code & 4095
    at = column(jnp.where(place < CAP, (code >> 12) * SOME + place - n * (CAP - SOME), -1))
    return jnp.where(iota((NB, FEW), 1) == at, 1.0, 0.0).astype(BF16)


def share(got, n):
    some = got[:, :SOME] if n == 0 else got[:, CAP - SOME:]
    return some.reshape(FEW, got.shape[2])


def arrivals(at_ref):
    code = at_ref[:, 2 * NB:]
    at = column(in_first(code))
    return jnp.where(iota((NB, 2 * CAP), 1) == at, 1.0, 0.0).astype(BF16), column(code) >= 0


def late(flag_ref, extra_ref, buffer, sem, first=True):
    @pl.when((flag_ref[0] < CAP) & first)
    def _():
        buffer[...] = jnp.zeros_like(buffer)

    @pl.when(flag_ref[0] >= CAP)
    def _():
        copy = pltpu.make_async_copy(extra_ref, buffer, sem)
        copy.start()
        copy.wait()

    return buffer


def panel_rows_kernel(where_ref, flag_ref, at_ref, got_ref, extra_ref, keep_ref, send_ref, tops_ref, more, sem):
    core = where_ref[1]
    more = late(flag_ref, extra_ref.at[:2 * NB, :128], more, sem)
    got = got_ref[...]
    first = pick(slots_of(at_ref, 0), split2(share(got, 0))) + more[:NB]
    second = pick(slots_of(at_ref, 1), split2(share(got, 1))) + more[NB:]
    left = iota((NB, 128), 1) < 64
    tops_ref[...] = jnp.where(left, first, second)
    swapped = jnp.where(left, second, first)
    upper = swapped[:HALF]
    lower = jnp.concatenate([swapped[HALF:], got[:2].reshape(2 * CAP, 128)], axis=0)
    keep_ref[...] = jnp.where(core == 0, upper, lower)
    send_ref[...] = jnp.where(core == 0, lower, upper)


def panel_rows(where, flag, at, got, extra):
    half = jax.ShapeDtypeStruct((HALF, 128), F32)
    return pl.pallas_call(
        panel_rows_kernel,
        in_specs=[SMEM] * 2 + [VMEM] * 2 + [ANY],
        out_specs=[VMEM] * 3,
        out_shape=[half, half, jax.ShapeDtypeStruct((NB, 128), F32)],
        scratch_shapes=[pltpu.VMEM((2 * NB, 128), F32), pltpu.SemaphoreType.DMA],
        compiler_params=pltpu.CompilerParams(vmem_limit_bytes=GRANT),
        name="panel_rows",
    )(where, flag, at, got, extra)


def fold_kernel(at_ref, lower_ref, one_ref, two_ref):
    for n, out in enumerate((one_ref, two_ref)):
        onehot = slots_of(at_ref, n)
        high, low = split2(lower_ref[n])
        out[0] = mm(high, onehot).astype(BF16)
        out[1] = mm(low, onehot).astype(BF16)


def fold(at, lower_inv):
    shape = jax.ShapeDtypeStruct((2, NB, FEW), BF16)
    return pl.pallas_call(
        fold_kernel, in_specs=[VMEM] * 2, out_specs=[VMEM] * 2, out_shape=[shape, shape], name="fold_slots"
    )(at, lower_inv)


def own_panels_kernel(where_ref, p0, p1, p2, p3, out_ref, gath):
    core, z = where_ref[1], where_ref[2]
    for s, piece in enumerate((p0, p1, p2, p3)):
        zz = lax.rem(z + 4 - s, 4)
        gath[zz, core] = piece[:128]
        gath[zz, 1 - core] = piece[128:]
    for n in range(2):
        half = [gath[c // 2, c % 2, 64 * n:64 * (n + 1)] for c in range(8)]
        out_ref[n] = jnp.transpose(jnp.concatenate(half, axis=0))


def own_panels(where, pieces):
    return pl.pallas_call(
        own_panels_kernel,
        in_specs=[SMEM] + [VMEM] * 4,
        out_specs=VMEM,
        out_shape=jax.ShapeDtypeStruct((2, NB, NB), F32),
        scratch_shapes=[pltpu.VMEM((4, 2, 128, NB), F32)],
        compiler_params=pltpu.CompilerParams(vmem_limit_bytes=GRANT),
        name="own_panels",
    )(where, *pieces)


def panel_math_kernel(where_ref, flag_ref, at_ref, tops_ref, whole_ref, extra_ref, k0, k1, k2, k3, p0, p1, p2, p3,
                      lower_ref, upper_ref, left_ref, pout_ref, gath, src, more, sem):
    me, core, z = where_ref[0], where_ref[1], where_ref[2]
    for s, (a, b) in enumerate(((k0, p0), (k1, p1), (k2, p2), (k3, p3))):
        zz = lax.rem(z + 4 - s, 4)
        gath[core, zz] = a[...]
        gath[1 - core, zz] = b[...]
    more = late(flag_ref, extra_ref, more, sem)
    left = iota((2 * HALF, 128), 1) < 64
    ones, twos = [], []
    for zz in range(4):
        a = jnp.concatenate([gath[0, zz, :HALF], gath[1, zz, HALF:]], axis=0)
        b = jnp.concatenate([gath[0, zz, HALF:], gath[1, zz, :HALF]], axis=0)
        ones.append(jnp.where(left, a, pltpu.roll(b, 64, 1)))
        twos.append(jnp.where(left, pltpu.roll(a, 64, 1), b))
    in_one, in_two = jnp.concatenate(ones, axis=1), jnp.concatenate(twos, axis=1)
    onehot, moved = arrivals(at_ref)
    top_two_one, top_one_two = in_one[:NB], in_two[:NB]
    own_one = jnp.where(moved, pick(onehot, split2(in_one[NB:])) + more[0], whole_ref[0])
    own_two = jnp.where(moved, pick(onehot, split2(in_two[NB:])) + more[1], whole_ref[1])
    own_one = jnp.where(me == 1, top_two_one, own_one)
    own_two = jnp.where(me == 1, 0.0, own_two)
    upper_one_inv = split2(upper_ref[0])
    lower_kept = dot3_upper(split2(own_one), upper_one_inv)
    lower_top = dot3_upper(split2(top_two_one), upper_one_inv)
    upper_panel = dot3_lower(split2(lower_ref[0]), split2(top_one_two))
    kept_parts = split2(lower_kept)
    updated = own_two - dot3(kept_parts, split2(upper_panel))
    lower_two = dot3_upper(split2(updated), split2(upper_ref[1]))
    left_ref[0], left_ref[1] = kept_parts
    left_ref[2], left_ref[3] = split2(lower_two)
    left_ref[4], left_ref[5] = split2(dot3_lower(split2(lower_ref[1]), split2(lower_top)))
    src[0] = lower_kept
    src[1] = jnp.where(me == 0, upper_panel, jnp.where(me == 1, updated, lower_two))
    at = pl.multiple_of(z * 128, 128)
    one = src[0, :, pl.ds(at, 128)]
    two = src[1, :, pl.ds(at, 128)]
    left = iota((NB, 128), 1) < 64
    mine = jnp.where(
        core == 0,
        jnp.where(left, one, pltpu.roll(two, 64, 1)),
        jnp.where(left, pltpu.roll(one, 64, 1), two),
    )
    tops = tops_ref[...]
    mine = jnp.where(left & (me == 0), tops, mine)
    mine = jnp.where(jnp.logical_not(left) & (me == 1), tops + mine, mine)
    pout_ref[...] = jnp.transpose(mine)


def panel_math(where, flag, at, tops, whole, extra, kept, other, lower_inv, upper_inv):
    return pl.pallas_call(
        panel_math_kernel,
        in_specs=[SMEM] * 2 + [VMEM] * 3 + [ANY] + [VMEM] * 10,
        out_specs=[VMEM] * 2,
        out_shape=[jax.ShapeDtypeStruct((6, NB, NB), BF16), jax.ShapeDtypeStruct((128, NB), F32)],
        scratch_shapes=[
            pltpu.VMEM((2, 4, 2 * HALF, 128), F32),
            pltpu.VMEM((2, NB, NB), F32),
            pltpu.VMEM((2, NB, NB), F32),
            pltpu.SemaphoreType.DMA,
        ],
        compiler_params=pltpu.CompilerParams(vmem_limit_bytes=GRANT),
        name="panel_math",
    )(where, flag, at, tops, whole, extra, *kept, *other, lower_inv, upper_inv)


WIDE = 256


def slab_kernel(where_ref, flag_ref, at_ref, got_ref, rows_ref, extra_ref, one_ref, two_ref, left_ref, out_ref,
                more, sem):
    me = where_ref[0]
    at = pl.multiple_of(pl.program_id(0) * WIDE, WIDE)
    more = late(flag_ref, extra_ref.at[:, pl.ds(at, WIDE)], more, sem, pl.program_id(0) == 0)
    got = got_ref[...]
    upper_one = dot3((one_ref[0], one_ref[1]), split2(share(got, 0))) + more[:NB]
    one = split2(upper_one)
    upper_two = (dot3((two_ref[0], two_ref[1]), split2(share(got, 1))) - dot3((left_ref[4], left_ref[5]), one)) + more[NB:2 * NB]

    @pl.when(me == 0)
    def _():
        out_ref[...] = upper_one

    @pl.when(me == 1)
    def _():
        out_ref[...] = upper_two

    @pl.when(me > 1)
    def _():
        onehot, moved = arrivals(at_ref)
        own = jnp.where(moved, pick(onehot, split2(got[:2].reshape(2 * CAP, WIDE))) + more[2 * NB:], rows_ref[...])
        two = split2(upper_two)
        out_ref[...] = own - dot3((left_ref[0], left_ref[1]), one) - dot3((left_ref[2], left_ref[3]), two)


def slab_math(where, flag, at, got, rows, extra, one, two, left):
    whole = lambda *shape: pl.BlockSpec(shape, lambda i: (0,) * len(shape))
    return pl.pallas_call(
        slab_kernel,
        grid=(NB // WIDE,),
        in_specs=[
            SMEM,
            SMEM,
            whole(1, 3 * NB),
            pl.BlockSpec((PEERS, CAP, WIDE), lambda i: (0, 0, i)),
            pl.BlockSpec((NB, WIDE), lambda i: (0, i)),
            ANY,
            whole(2, NB, FEW),
            whole(2, NB, FEW),
            whole(6, NB, NB),
        ],
        out_specs=pl.BlockSpec((NB, WIDE), lambda i: (0, i)),
        out_shape=jax.ShapeDtypeStruct((NB, NB), F32),
        scratch_shapes=[pltpu.VMEM((3 * NB, WIDE), F32), pltpu.SemaphoreType.DMA],
        name="slab_math",
    )(where, flag, at, got, rows, extra, one, two, left)


def mark_kernel(in_ref, out_ref):
    out_ref[0] = in_ref[0]


def mark(x):
    return pl.pallas_call(
        mark_kernel, in_specs=[SMEM], out_specs=SMEM, out_shape=jax.ShapeDtypeStruct((1,), jnp.int32), name="mark"
    )(x)


def exchange(blocks):
    width = blocks.shape[1]
    return lax.all_to_all(blocks.reshape(PEERS, CAP, width), RD, 0, 0)


def unused_kernel(*refs):
    pass


def unwritten(*shapes):
    return pl.pallas_call(
        unused_kernel,
        out_specs=[ANY] * len(shapes),
        out_shape=[jax.ShapeDtypeStruct(shape, F32) for shape in shapes],
        name="unwritten",
    )()


def late_pack_kernel(base_ref, codes_ref, panel_ref, rows_ref, out_ref):
    k = iota((CAP, NB), 0) + base_ref[0]
    picked = (k == codes_ref[0:1]) | ((k + pl.program_id(0) * 4096) == codes_ref[1:2])
    onehot = jnp.where(picked, 1.0, 0.0).astype(BF16)
    out_ref[:, :128] = pick_t(onehot, split2(panel_ref[...]))
    out_ref[:, 128:] = pick(onehot, split2(rows_ref[...]))


def late_pack(base, codes, panel_t, slab):
    whole = lambda *shape: pl.BlockSpec(shape, lambda i: (0,) * len(shape))
    return pl.pallas_call(
        late_pack_kernel,
        grid=(PEERS,),
        in_specs=[SMEM, whole(8, NB), whole(128, NB), whole(NB, NB)],
        out_specs=pl.BlockSpec((CAP, 128 + NB), lambda i: (i, 0)),
        out_shape=jax.ShapeDtypeStruct((SLOTS, 128 + NB), F32),
        name="late_pack",
    )(base, codes, panel_t, slab)


def late_place_kernel(base_ref, every_ref, got_ref, old_ref, out_ref):
    code = column(every_ref[...])
    place = (code & 4095) - base_ref[0]
    now = (code >= 0) & (place >= 0) & (place < CAP)
    at = jnp.where(now, (code >> 12) * CAP + place, -1)
    onehot = jnp.where(iota((128, SLOTS), 1) == at, 1.0, 0.0).astype(BF16)
    old = jnp.where(base_ref[0] == CAP, 0.0, old_ref[...])
    out_ref[...] = jnp.where(now, pick(onehot, split2(got_ref[...])), old)


def late_place(base, every, got, old):
    block = pl.BlockSpec((128, 128 + NB), lambda i: (i, 0))
    return pl.pallas_call(
        late_place_kernel,
        grid=(12,),
        in_specs=[
            SMEM,
            pl.BlockSpec((1, 128), lambda i: (0, i)),
            pl.BlockSpec((SLOTS, 128 + NB), lambda i: (0, 0)),
            block,
        ],
        out_specs=block,
        out_shape=jax.ShapeDtypeStruct((3 * NB, 128 + NB), F32),
        name="late_place",
    )(base, every, got, old)


def late_product_kernel(lower_ref, rows_ref, out_ref):
    n = pl.program_id(0)

    @pl.when(n < 8)
    def _():
        out_ref[...] = dot3(split2(lower_ref[0]), split2(rows_ref[:, 128:]))

    @pl.when(n >= 8)
    def _():
        at = pl.multiple_of(lax.rem(n, 4) * 128, 128)
        out_ref[...] = rows_ref[pl.ds(at, 128), 128:]


def late_product(lower_inv, rows):
    return pl.pallas_call(
        late_product_kernel,
        grid=(12,),
        in_specs=[
            pl.BlockSpec((1, 128, NB), lambda i: (lax.min(i // 4, 1), i % 4, 0)),
            pl.BlockSpec((NB, 128 + NB), lambda i: (i // 4, 0)),
        ],
        out_specs=pl.BlockSpec((128, NB), lambda i: (i, 0)),
        out_shape=jax.ShapeDtypeStruct((3 * NB, NB), F32),
        name="late_product",
    )(lower_inv, rows)


def late_panel_kernel(in_ref, out_ref):
    left = iota((NB, 128), 1) < 64
    a, b = in_ref[0], in_ref[1]
    out_ref[0] = jnp.where(left, a, pltpu.roll(b, 64, 1))
    out_ref[1] = jnp.where(left, pltpu.roll(a, 64, 1), b)


def late_panel(pieces):
    return pl.pallas_call(
        late_panel_kernel,
        grid=(4,),
        in_specs=[pl.BlockSpec((2, NB, 128), lambda i: (i, 0, 0))],
        out_specs=pl.BlockSpec((2, NB, 128), lambda i: (0, 0, i)),
        out_shape=jax.ShapeDtypeStruct((2, NB, NB), F32),
        name="late_panel",
    )(pieces)


def late_exchange(blocks, me):
    ring = [(i, (i + 1) % PEERS) for i in range(PEERS)]

    def turn(t, state):
        held, got = state
        mine = lax.dynamic_slice_in_dim(held, me * CAP, CAP, 0)
        got = lax.dynamic_update_slice_in_dim(got, mine, (me - t) % PEERS * CAP, 0)
        return lax.ppermute(held, RD, ring), got

    return lax.fori_loop(0, PEERS, turn, (blocks, jnp.zeros(blocks.shape, F32)))[1]


def late_gather(rows, col):
    ring = [(i, (i + 1) % 8) for i in range(8)]

    def turn(t, state):
        held, got = state
        got = lax.dynamic_update_slice_in_dim(got, held[None], (col - t) % 8, 0)
        return lax.ppermute(held, "col", ring), got

    return lax.fori_loop(0, 8, turn, (rows, jnp.zeros((8, *rows.shape), F32)))[1]


def further_rounds(most, codes, every, panel_t, slab, lower_inv, me, col):
    def turn(state):
        r, rows = state[:2]
        base = (r * CAP).reshape(1)
        got = late_exchange(late_pack(base, codes, panel_t, slab), me)
        rows = late_place(base, every, got, rows)
        wide = late_panel(late_gather(rows[2 * NB:, :128], col))
        return r + 1, rows, wide, late_product(lower_inv, rows)

    start = (jnp.int32(1), *unwritten((3 * NB, 128 + NB), (2, NB, NB), (3 * NB, NB)))
    return lax.while_loop(lambda s: s[0] * CAP <= most, turn, start)[1:]


def partner(x):
    return lax.ppermute(x, "col", [(c, c ^ 1) for c in range(8)])


def shift(x, by):
    return lax.ppermute(x, "col", [(c, (c // 2 + by) % 4 * 2 + c % 2) for c in range(8)])


def body(panels, slab, pivot_one, pivot_two, lower_inv, upper_inv):
    me = lax.axis_index(RD)
    col = lax.axis_index("col")
    where = jnp.stack([me, col % 2, col // 2, col]).astype(jnp.int32)
    panel_t = jnp.swapaxes(panels, 1, 2).reshape(128, NB)
    panel_pair = jnp.concatenate([panel_t, partner(panel_t)], axis=0)
    codes, every, most, blocks = make_plan(where, pivot_one, pivot_two, panel_t)
    got_panel = exchange(blocks)
    pieces = [panel_pair] + [shift(panel_pair, by) for by in (1, 2, 3)]
    whole = own_panels(where, pieces)
    blocks = pack(codes, slab)
    most = mark(most)
    late_rows, late_own, late_slab = further_rounds(most[0], codes, every, panel_t, slab, lower_inv, me, col)
    got_slab = exchange(blocks)
    keep, send, tops = panel_rows(where, most, every, got_panel, late_rows)
    pair = jnp.concatenate([keep, partner(send)], axis=0)
    shifted = [shift(pair, by) for by in (1, 2, 3)]
    one, two = fold(every, lower_inv)
    shifted, one, two = lax.optimization_barrier((shifted, one, two))
    kept = [pair] + shifted
    other = [partner(x) for x in kept]
    left, panel_out = panel_math(where, most, every, tops, whole, late_own, kept, other, lower_inv, upper_inv)
    slab_out = slab_math(where, most, every, got_slab, slab, late_slab, one, two, left)
    return jnp.swapaxes(panel_out.reshape(2, 64, NB), 1, 2), slab_out


def solution(mesh):
    placed = (P(None, RD, "col"), P(RD, "col"), P(), P(), P(), P())
    return jax.shard_map(
        body,
        mesh=mesh,
        in_specs=placed,
        out_specs=(P(None, RD, "col"), P(RD, "col")),
        check_vma=False,
    )
```

profile of v0, /device:TPU:5, one launch (start us, length us, event | category | flops | bytes accessed | tf_op | source)
XLA Modules:
  0.0 108.0 jit_solution(13467931178644566888)
XLA Ops:
  0.7 0.6 pad_add_fusion.where_ref
  1.3 4.4 %make_plan.1 = (s32[8,512]{1,0:T(8,128)S(1)}, s32[1,1536]{1,0:T(1,128)S(1)}, s32[1]{0:T(128)}, f32[1536,128]{1,0:T(8,128)}) custom-call(s32[4]{0:T(128)} %pad_add_fusion.where_ref, s32[1,512]{1,0:T(1,128)} %bitcast.28, s32[1,512]{1,0:T(1,128)} %bitcast.29, f32[128,512]{1,0:T(8,128)} %bitcast.22), custom_call_target="tpu_custom_call" | custom-call | tf_op jit(solution)/shard_map/make_plan/pallas_call | solution.py:162
  5.7 6.9 %all-to-all-start = ((f32[16,96,128]{2,1,0:T(8,128)}), f32[16,96,128]{2,1,0:T(8,128)S(1)}, u32[]{:S(2)}, u32[]{:S(2)}) async-start(f32[16,96,128]{2,1,0:T(8,128)} %bitcast.27), calls=%async_computation | async-start | bytes 1572864 | tf_op jit(solution)/shard_map/all_to_all | solution.py:429
  12.6 1.2 %collective-permute-start.2 = (f32[128,512]{1,0:T(8,128)}, f32[128,512]{1,0:T(8,128)}, u32[]{:S(2)}, u32[]{:S(2)}) collective-permute-start(f32[128,512]{1,0:T(8,128)} %bitcast.23), channel_id=1, source_target_pairs={{0,4},{4,0},{8,12},{12,8},{16,20},{20,16},{24,28},{28,24},{1,5},{5... | collective-permute-start | bytes 786440 | tf_op jit(solution)/shard_map/ppermute | solution.py:574
  13.9 1.2 %mark.1.flag_ref = s32[1]{0:T(128)} custom-call(s32[1]{0:T(128)} %get-tuple-element.525.in_ref), custom_call_target="tpu_custom_call" | custom-call | tf_op jit(solution)/shard_map/mark/pallas_call | solution.py:422
  15.1 5.0 %pack_rows.1 = f32[1536,512]{1,0:T(8,128)} custom-call(s32[8,512]{1,0:T(8,128)S(1)} %get-tuple-element.808.codes_ref, f32[512,512]{1,0:T(8,128)} %rows_ref.3), custom_call_target="tpu_custom_call" | custom-call | tf_op jit(solution)/shard_map/pack_rows/pallas_call | solution.py:190
  20.0 4.8 %all-to-all-done.got_ref = f32[16,96,128]{2,1,0:T(8,128)S(1)} async-done(((f32[16,96,128]{2,1,0:T(8,128)}), f32[16,96,128]{2,1,0:T(8,128)S(1)}, u32[]{:S(2)}, u32[]{:S(2)}) %all-to-all-start) | async-done | bytes 786464 | tf_op jit(solution)/shard_map/all_to_all | solution.py:429
  24.8 5.5 %all-to-all-start.1 = ((f32[16,96,512]{2,1,0:T(8,128)}), f32[16,96,512]{2,1,0:T(8,128)}, u32[]{:S(2)}, u32[]{:S(2)}) async-start(f32[16,96,512]{2,1,0:T(8,128)} %bitcast.26), calls=%async_computation.1 | async-start | bytes 6291456 | tf_op jit(solution)/shard_map/all_to_all | solution.py:429
  30.3 0.0 copy-done.6
  30.3 0.0 copy-done.8
  30.3 0.0 copy-start.4
  30.3 0.6 while.66
  31.0 0.0 copy-done.4
  31.0 2.3 %panel_rows.1 = (f32[352,128]{1,0:T(8,128)S(1)}, f32[352,128]{1,0:T(8,128)S(1)}, f32[512,128]{1,0:T(8,128)S(1)}) custom-call(s32[4]{0:T(128)S(1)} %copy-done.4, s32[1]{0:T(128)} %mark.1.flag_ref, s32[1,1536]{1,0:T(1,128)S(1)} %get-tuple-element.940, f32[16,96,128]{2,1,0:T(8,128)S(1)} %all-to-all-done.got_ref, f32[1536,640]{1,0:T(8,128)} %get-tuple-element.931), custom_call_target="tpu_custom_call" | custom-call | tf_op jit(solution)/shard_map/panel_rows/pallas_call | solution.py:250
  33.3 0.0 copy-start.2
  33.3 2.6 %collective-permute-start.6 = (f32[352,128]{1,0:T(8,128)S(1)}, f32[352,128]{1,0:T(8,128)S(1)}, u32[]{:S(2)}, u32[]{:S(2)}) collective-permute-start(f32[352,128]{1,0:T(8,128)S(1)} %get-tuple-element.536), channel_id=1, source_target_pairs={{0,4},{4,0},{8,12},{12,8},{16,20},{20,16},{24,28},{28,24},{1,5},{5... | collective-permute-start | bytes 540680 | tf_op jit(solution)/shard_map/ppermute | solution.py:574
  35.9 0.0 collective-permute-done.2
  35.9 1.0 pad_maximum_fusion.p0
  36.9 0.0 collective-permute-done.6
  37.0 0.0 copy-start.1
  37.0 1.7 %collective-permute-start.7 = (f32[704,128]{1,0:T(8,128)S(1)}, f32[704,128]{1,0:T(8,128)}, u32[]{:S(2)}, u32[]{:S(2)}) collective-permute-start(f32[704,128]{1,0:T(8,128)S(1)} %constant_dynamic-update-slice_fusion.k0), channel_id=1, source_target_pairs={{0,8},{4,12},{8,16},{12,20},{16,24},{20,28},{24,0},{28,4},{1,9},{5... | collective-permute-start | bytes 1081352 | tf_op jit(solution)/shard_map/ppermute | solution.py:578
  38.7 1.6 %collective-permute-start.3 = (f32[256,512]{1,0:T(8,128)S(1)}, f32[256,512]{1,0:T(8,128)S(1)}, u32[]{:S(2)}, u32[]{:S(2)}) collective-permute-start(f32[256,512]{1,0:T(8,128)S(1)} %pad_maximum_fusion.p0), channel_id=1, source_target_pairs={{0,8},{4,12},{8,16},{12,20},{16,24},{20,28},{24,0},{28,4},{1,9},{5... | collective-permute-start | bytes 1572872 | tf_op jit(solution)/shard_map/ppermute | solution.py:578
  40.3 1.7 %collective-permute-start.4 = (f32[256,512]{1,0:T(8,128)S(1)}, f32[256,512]{1,0:T(8,128)}, u32[]{:S(2)}, u32[]{:S(2)}) collective-permute-start(f32[256,512]{1,0:T(8,128)S(1)} %pad_maximum_fusion.p0), channel_id=1, source_target_pairs={{0,16},{4,20},{8,24},{12,28},{16,0},{20,4},{24,8},{28,12},{1,17},{... | collective-permute-start | bytes 1572872 | tf_op jit(solution)/shard_map/ppermute | solution.py:578
  42.1 1.2 %collective-permute-start.8 = (f32[704,128]{1,0:T(8,128)S(1)}, f32[704,128]{1,0:T(8,128)}, u32[]{:S(2)}, u32[]{:S(2)}) collective-permute-start(f32[704,128]{1,0:T(8,128)S(1)} %constant_dynamic-update-slice_fusion.k0), channel_id=1, source_target_pairs={{0,16},{4,20},{8,24},{12,28},{16,0},{20,4},{24,8},{28,12},{1,17},{... | collective-permute-start | bytes 1081352 | tf_op jit(solution)/shard_map/ppermute | solution.py:578
  43.3 1.0 collective-permute-start.9
  44.3 5.0 %collective-permute-done.7.k1 = f32[704,128]{1,0:T(8,128)} collective-permute-done((f32[704,128]{1,0:T(8,128)S(1)}, f32[704,128]{1,0:T(8,128)}, u32[]{:S(2)}, u32[]{:S(2)}) %collective-permute-start.7) | collective-permute-done | bytes 360480 | tf_op jit(solution)/shard_map/ppermute | solution.py:578
  49.3 0.0 copy-done.2
  49.3 1.2 %collective-permute-start.5 = (f32[256,512]{1,0:T(8,128)S(1)}, f32[256,512]{1,0:T(8,128)}, u32[]{:S(2)}, u32[]{:S(2)}) collective-permute-start(f32[256,512]{1,0:T(8,128)S(1)} %pad_maximum_fusion.p0), channel_id=1, source_target_pairs={{0,24},{4,28},{8,0},{12,4},{16,8},{20,12},{24,16},{28,20},{1,25},{... | collective-permute-start | bytes 1572872 | tf_op jit(solution)/shard_map/ppermute | solution.py:578
  50.5 5.8 %fold_slots.1 = (bf16[2,512,1024]{2,1,0:T(8,128)(2,1)}, bf16[2,512,1024]{2,1,0:T(8,128)(2,1)}) custom-call(s32[1,1536]{1,0:T(1,128)S(1)} %get-tuple-element.940, f32[2,512,512]{2,1,0:T(8,128)} %get-tuple-element.942), custom_call_target="tpu_custom_call" | custom-call | tf_op jit(solution)/shard_map/fold_slots/pallas_call | solution.py:271
  56.3 24.1 %collective-permute-done.8.k2 = f32[704,128]{1,0:T(8,128)} collective-permute-done((f32[704,128]{1,0:T(8,128)S(1)}, f32[704,128]{1,0:T(8,128)}, u32[]{:S(2)}, u32[]{:S(2)}) %collective-permute-start.8) | collective-permute-done | bytes 360480 | tf_op jit(solution)/shard_map/ppermute | solution.py:578
  80.4 1.2 %collective-permute-start.10 = (f32[704,128]{1,0:T(8,128)S(1)}, f32[704,128]{1,0:T(8,128)S(1)}, u32[]{:S(2)}, u32[]{:S(2)}) collective-permute-start(f32[704,128]{1,0:T(8,128)S(1)} %constant_dynamic-update-slice_fusion.k0), channel_id=1, source_target_pairs={{0,4},{4,0},{8,12},{12,8},{16,20},{20,16},{24,28},{28,24},{1,5},{5... | collective-permute-start | bytes 1081352 | tf_op jit(solution)/shard_map/ppermute | solution.py:574
  81.6 0.0 collective-permute-done.9.k3
  81.7 0.0 collective-permute-start.11
  81.7 0.0 collective-permute-done.3.p1
  81.7 0.5 collective-permute-start.12
  82.2 0.0 collective-permute-done.4.p2
  82.2 0.1 collective-permute-start.13
  82.3 0.0 collective-permute-done.5.p3
  82.3 1.9 %own_panels.1.whole_ref = f32[2,512,512]{2,1,0:T(8,128)S(1)} custom-call(s32[4]{0:T(128)S(1)} %copy-done.4, f32[256,512]{1,0:T(8,128)S(1)} %pad_maximum_fusion.p0, f32[256,512]{1,0:T(8,128)S(1)} %collective-permute-done.3.p1, f32[256,512]{1,0:T(8,128)} %collective-permute-done.4.p2, f32[256,512]{1,0:T(8,128)} %collective-permute-done.5.p3), custom_call_target="tpu_custom_call" | custom-call | tf_op jit(solution)/shard_map/own_panels/pallas_call | solution.py:288
  84.2 0.0 collective-permute-done.10.p0
  84.2 0.0 collective-permute-done.11.p1
  84.2 0.0 collective-permute-done.12.p2
  84.2 0.3 collective-permute-done.13.p3
  84.6 0.0 copy-done.1
  84.6 8.8 %panel_math.1 = (bf16[6,512,512]{2,1,0:T(8,128)(2,1)S(1)}, f32[128,512]{1,0:T(8,128)}) custom-call(s32[4]{0:T(128)S(1)} %copy-done.4, s32[1]{0:T(128)} %mark.1.flag_ref, s32[1,1536]{1,0:T(1,128)S(1)} %get-tuple-element.940, f32[512,128]{1,0:T(8,128)S(1)} %copy-done.3, f32[2,512,512]{2,1,0:T(8,128)S(1)} %own_panels.1.whole_ref, ...), custom_call_target="tpu_custom_call" | custom-call | tf_op jit(solution)/shard_map/panel_math/pallas_call | solution.py:349
  93.4 1.6 %copy-done = bf16[6,512,512]{2,1,0:T(8,128)(2,1)} copy-done((bf16[6,512,512]{2,1,0:T(8,128)(2,1)}, bf16[6,512,512]{2,1,0:T(8,128)(2,1)S(1)}, u32[]{:S(2)}) %copy-start) | copy-done | bytes 3145752
  95.1 0.0 all-to-all-done.1.got_ref
  95.1 12.8 %slab_math.1 = f32[512,512]{1,0:T(8,128)} custom-call(s32[4]{0:T(128)} %pad_add_fusion.where_ref, s32[1]{0:T(128)} %mark.1.flag_ref, s32[1,1536]{1,0:T(1,128)S(1)} %get-tuple-element.940, f32[16,96,512]{2,1,0:T(8,128)} %all-to-all-done.1.got_ref, f32[512,512]{1,0:T(8,128)} %rows_ref.3, f32[1536,512]{1,0:T(8,128)} %get-tuple-element.933, ...), custom_call_target="tpu_custom_call" | custom-call | tf_op jit(solution)/shard_map/slab_math/pallas_call | solution.py:396
  (10 shorter events, 0.0 us)
Async XLA Ops:
  5.7 19.1 %all-to-all-start = ((f32[16,96,128]{2,1,0:T(8,128)}), f32[16,96,128]{2,1,0:T(8,128)S(1)}, u32[]{:S(2)}, u32[]{:S(2)}) async-start(f32[16,96,128]{2,1,0:T(8,128)} %bitcast.27), calls=%async_computation | async-start | bytes 1572864 | tf_op jit(solution)/shard_map/all_to_all | solution.py:429
  12.6 23.3 %collective-permute-start.2 = (f32[128,512]{1,0:T(8,128)}, f32[128,512]{1,0:T(8,128)}, u32[]{:S(2)}, u32[]{:S(2)}) collective-permute-start(f32[128,512]{1,0:T(8,128)} %bitcast.23), channel_id=1, source_target_pairs={{0,4},{4,0},{8,12},{12,8},{16,20},{20,16},{24,28},{28,24},{1,5},{5... | collective-permute-start | bytes 786440 | tf_op jit(solution)/shard_map/ppermute | solution.py:574
  24.8 5.5 %copy-start.6 = (f32[512,512]{1,0:T(8,128)S(1)}, f32[512,512]{1,0:T(8,128)}, u32[]{:S(2)}) copy-start(f32[512,512]{1,0:T(8,128)} %rows_ref.3) | copy-start | bytes 3145732
  24.8 5.5 %copy-start.8 = (f32[2,512,64]{1,2,0:T(8,128)S(1)}, f32[2,512,64]{1,2,0:T(8,128)}, u32[]{:S(2)}) copy-start(f32[2,512,64]{1,2,0:T(8,128)} %param.12) | copy-start | bytes 786436
  24.8 70.2 %all-to-all-start.1 = ((f32[16,96,512]{2,1,0:T(8,128)}), f32[16,96,512]{2,1,0:T(8,128)}, u32[]{:S(2)}, u32[]{:S(2)}) async-start(f32[16,96,512]{2,1,0:T(8,128)} %bitcast.26), calls=%async_computation.1 | async-start | bytes 6291456 | tf_op jit(solution)/shard_map/all_to_all | solution.py:429
  30.3 0.7 copy-start.4
  33.3 16.0 %copy-start.2 = (f32[512,128]{1,0:T(8,128)}, f32[512,128]{1,0:T(8,128)S(1)}, u32[]{:S(2)}) copy-start(f32[512,128]{1,0:T(8,128)S(1)} %get-tuple-element.533.tops_ref) | copy-start | bytes 786436
  33.3 3.6 %collective-permute-start.6 = (f32[352,128]{1,0:T(8,128)S(1)}, f32[352,128]{1,0:T(8,128)S(1)}, u32[]{:S(2)}, u32[]{:S(2)}) collective-permute-start(f32[352,128]{1,0:T(8,128)S(1)} %get-tuple-element.536), channel_id=1, source_target_pairs={{0,4},{4,0},{8,12},{12,8},{16,20},{20,16},{24,28},{28,24},{1,5},{5... | collective-permute-start | bytes 540680 | tf_op jit(solution)/shard_map/ppermute | solution.py:574
  37.0 47.6 %copy-start.1 = (f32[2,512,512]{2,1,0:T(8,128)S(1)}, f32[2,512,512]{2,1,0:T(8,128)}, u32[]{:S(2)}) copy-start(f32[2,512,512]{2,1,0:T(8,128)} %upper_ref.1) | copy-start | bytes 6291460
  37.0 12.3 %collective-permute-start.7 = (f32[704,128]{1,0:T(8,128)S(1)}, f32[704,128]{1,0:T(8,128)}, u32[]{:S(2)}, u32[]{:S(2)}) collective-permute-start(f32[704,128]{1,0:T(8,128)S(1)} %constant_dynamic-update-slice_fusion.k0), channel_id=1, source_target_pairs={{0,8},{4,12},{8,16},{12,20},{16,24},{20,28},{24,0},{28,4},{1,9},{5... | collective-permute-start | bytes 1081352 | tf_op jit(solution)/shard_map/ppermute | solution.py:578
  38.7 43.0 %collective-permute-start.3 = (f32[256,512]{1,0:T(8,128)S(1)}, f32[256,512]{1,0:T(8,128)S(1)}, u32[]{:S(2)}, u32[]{:S(2)}) collective-permute-start(f32[256,512]{1,0:T(8,128)S(1)} %pad_maximum_fusion.p0), channel_id=1, source_target_pairs={{0,8},{4,12},{8,16},{12,20},{16,24},{20,28},{24,0},{28,4},{1,9},{5... | collective-permute-start | bytes 1572872 | tf_op jit(solution)/shard_map/ppermute | solution.py:578
  40.3 41.8 %collective-permute-start.4 = (f32[256,512]{1,0:T(8,128)S(1)}, f32[256,512]{1,0:T(8,128)}, u32[]{:S(2)}, u32[]{:S(2)}) collective-permute-start(f32[256,512]{1,0:T(8,128)S(1)} %pad_maximum_fusion.p0), channel_id=1, source_target_pairs={{0,16},{4,20},{8,24},{12,28},{16,0},{20,4},{24,8},{28,12},{1,17},{... | collective-permute-start | bytes 1572872 | tf_op jit(solution)/shard_map/ppermute | solution.py:578
  42.1 38.3 %collective-permute-start.8 = (f32[704,128]{1,0:T(8,128)S(1)}, f32[704,128]{1,0:T(8,128)}, u32[]{:S(2)}, u32[]{:S(2)}) collective-permute-start(f32[704,128]{1,0:T(8,128)S(1)} %constant_dynamic-update-slice_fusion.k0), channel_id=1, source_target_pairs={{0,16},{4,20},{8,24},{12,28},{16,0},{20,4},{24,8},{28,12},{1,17},{... | collective-permute-start | bytes 1081352 | tf_op jit(solution)/shard_map/ppermute | solution.py:578
  43.3 38.4 %collective-permute-start.9 = (f32[704,128]{1,0:T(8,128)S(1)}, f32[704,128]{1,0:T(8,128)}, u32[]{:S(2)}, u32[]{:S(2)}) collective-permute-start(f32[704,128]{1,0:T(8,128)S(1)} %constant_dynamic-update-slice_fusion.k0), channel_id=1, source_target_pairs={{0,24},{4,28},{8,0},{12,4},{16,8},{20,12},{24,16},{28,20},{1,25},{... | collective-permute-start | bytes 1081352 | tf_op jit(solution)/shard_map/ppermute | solution.py:578
  49.3 32.9 %collective-permute-start.5 = (f32[256,512]{1,0:T(8,128)S(1)}, f32[256,512]{1,0:T(8,128)}, u32[]{:S(2)}, u32[]{:S(2)}) collective-permute-start(f32[256,512]{1,0:T(8,128)S(1)} %pad_maximum_fusion.p0), channel_id=1, source_target_pairs={{0,24},{4,28},{8,0},{12,4},{16,8},{20,12},{24,16},{28,20},{1,25},{... | collective-permute-start | bytes 1572872 | tf_op jit(solution)/shard_map/ppermute | solution.py:578
  56.3 28.3 %copy-start.3 = (f32[512,128]{1,0:T(8,128)S(1)}, f32[512,128]{1,0:T(8,128)}, u32[]{:S(2)}) copy-start(f32[512,128]{1,0:T(8,128)} %copy-done.2) | copy-start | bytes 786436
  56.3 28.3 %copy-start.5 = (f32[2,512,512]{2,1,0:T(8,128)S(1)}, f32[2,512,512]{2,1,0:T(8,128)}, u32[]{:S(2)}) copy-start(f32[2,512,512]{2,1,0:T(8,128)} %get-tuple-element.942) | copy-start | bytes 6291460
  80.4 3.8 %collective-permute-start.10 = (f32[704,128]{1,0:T(8,128)S(1)}, f32[704,128]{1,0:T(8,128)S(1)}, u32[]{:S(2)}, u32[]{:S(2)}) collective-permute-start(f32[704,128]{1,0:T(8,128)S(1)} %constant_dynamic-update-slice_fusion.k0), channel_id=1, source_target_pairs={{0,4},{4,0},{8,12},{12,8},{16,20},{20,16},{24,28},{28,24},{1,5},{5... | collective-permute-start | bytes 1081352 | tf_op jit(solution)/shard_map/ppermute | solution.py:574
  81.7 2.6 %collective-permute-start.11 = (f32[704,128]{1,0:T(8,128)}, f32[704,128]{1,0:T(8,128)S(1)}, u32[]{:S(2)}, u32[]{:S(2)}) collective-permute-start(f32[704,128]{1,0:T(8,128)} %collective-permute-done.7.k1), channel_id=1, source_target_pairs={{0,4},{4,0},{8,12},{12,8},{16,20},{20,16},{24,28},{28,24},{1,5},{5... | collective-permute-start | bytes 1081352 | tf_op jit(solution)/shard_map/ppermute | solution.py:574
  81.7 2.6 %collective-permute-start.12 = (f32[704,128]{1,0:T(8,128)}, f32[704,128]{1,0:T(8,128)S(1)}, u32[]{:S(2)}, u32[]{:S(2)}) collective-permute-start(f32[704,128]{1,0:T(8,128)} %collective-permute-done.8.k2), channel_id=1, source_target_pairs={{0,4},{4,0},{8,12},{12,8},{16,20},{20,16},{24,28},{28,24},{1,5},{5... | collective-permute-start | bytes 1081352 | tf_op jit(solution)/shard_map/ppermute | solution.py:574
  82.2 2.4 %collective-permute-start.13 = (f32[704,128]{1,0:T(8,128)}, f32[704,128]{1,0:T(8,128)S(1)}, u32[]{:S(2)}, u32[]{:S(2)}) collective-permute-start(f32[704,128]{1,0:T(8,128)} %collective-permute-done.9.k3), channel_id=1, source_target_pairs={{0,4},{4,0},{8,12},{12,8},{16,20},{20,16},{24,28},{28,24},{1,5},{5... | collective-permute-start | bytes 1081352 | tf_op jit(solution)/shard_map/ppermute | solution.py:574
  93.4 1.6 %copy-start = (bf16[6,512,512]{2,1,0:T(8,128)(2,1)}, bf16[6,512,512]{2,1,0:T(8,128)(2,1)S(1)}, u32[]{:S(2)}) copy-start(bf16[6,512,512]{2,1,0:T(8,128)(2,1)S(1)} %get-tuple-element.546.left_ref) | copy-start | bytes 9437188
where the time goes:
time: 109 us; the launch traced here: 108 us
  Pallas kernels  42.2 us (39%)
  waiting for transfers between devices  34.3 us (31%)
  starting transfers between devices  26.6 us (24%)
  local copies, waits for them, and re-layouts  1.68 us (2%)
  other arithmetic  1.63 us (1%)
    ppermute x6, waiting for transfers between devices, shift(): lax.ppermute(x, 'col', [(c, (c // 2 + by) % 4 * 2 + c % 2) for c in range...  29.1 us
    pallas_call x1, Pallas kernels, slab_math(): pl.pallas_call(slab_kernel, grid=(NB // WIDE,), in_specs=[SMEM, SMEM, who...  12.8 us
    all_to_all x2, starting transfers between devices, exchange(): return lax.all_to_all(blocks.reshape(PEERS, CAP, width), RD, 0, 0)  12.4 us
    pallas_call x1, Pallas kernels, panel_math(): pl.pallas_call(panel_math_kernel, in_specs=[SMEM] * 2 + [VMEM] * 3 + [ANY...  8.85 us
    ppermute x6, starting transfers between devices, shift(): lax.ppermute(x, 'col', [(c, (c // 2 + by) % 4 * 2 + c % 2) for c in range...  8.53 us
    pallas_call x1, Pallas kernels, fold(): pl.pallas_call(fold_kernel, in_specs=[VMEM] * 2, out_specs=[VMEM] * 2, ou...  5.77 us
    ppermute x6, starting transfers between devices, partner(): return lax.ppermute(x, 'col', [(c, c ^ 1) for c in range(8)])  5.66 us
    pallas_call x1, Pallas kernels, pack(): pl.pallas_call(pack_kernel, grid=(4,), in_specs=[pl.BlockSpec((8, NB), la...  4.98 us
  transfers between devices with their start and end apart: 14, of which 4 were waited for; matrix products, arithmetic and copies ran while one was open for 1% of the time, Pallas kernels for 23%

commit v1 on v0

--- a/solution.py
+++ b/solution.py
@@ -414,16 +414,6 @@
     )(where, flag, at, got, rows, extra, one, two, left)
 
 
-def mark_kernel(in_ref, out_ref):
-    out_ref[0] = in_ref[0]
-
-
-def mark(x):
-    return pl.pallas_call(
-        mark_kernel, in_specs=[SMEM], out_specs=SMEM, out_shape=jax.ShapeDtypeStruct((1,), jnp.int32), name="mark"
-    )(x)
-
-
 def exchange(blocks):
     width = blocks.shape[1]
     return lax.all_to_all(blocks.reshape(PEERS, CAP, width), RD, 0, 0)
@@ -589,7 +579,6 @@
     pieces = [panel_pair] + [shift(panel_pair, by) for by in (1, 2, 3)]
     whole = own_panels(where, pieces)
     blocks = pack(codes, slab)
-    most = mark(most)
     late_rows, late_own, late_slab = further_rounds(most[0], codes, every, panel_t, slab, lower_inv, me, col)
     got_slab = exchange(blocks)
     keep, send, tops = panel_rows(where, most, every, got_panel, late_rows)

time: 109 us -> 108 us (level)
  Pallas kernels: 42.2 us -> 41 us
  waiting for transfers between devices: 34.3 us -> 35.5 us
    all_to_all x2, waiting for transfers between devices: 4.77 us -> 6.01 us  [exchange(): return lax.all_to_all(blocks.reshape(PEERS, CAP, width), RD, 0, 0)]
    pallas_call x1 -> x0, Pallas kernels: 1.21 us -> none  [mark(): pl.pallas_call(mark_kernel, in_specs=[SMEM], out_specs=SMEM, out_shape=ja...]
  transfers between devices with their start and end apart: 14 -> 14, of which waited for: 4 -> 4; matrix products, arithmetic and copies ran while one was open for 1% -> 1% of each run, Pallas kernels for 23% -> 22%
where the time goes in v1:
time: 108 us
  Pallas kernels  41 us (38%)
  waiting for transfers between devices  35.5 us (33%)
  starting transfers between devices  26.6 us (25%)
  local copies, waits for them, and re-layouts  1.68 us (2%)
  other arithmetic  1.63 us (2%)
    ppermute x6, waiting for transfers between devices, shift(): lax.ppermute(x, 'col', [(c, (c // 2 + by) % 4 * 2 + c % 2) for c in range...  29.1 us
    pallas_call x1, Pallas kernels, slab_math(): pl.pallas_call(slab_kernel, grid=(NB // WIDE,), in_specs=[SMEM, SMEM, who...  12.8 us
    all_to_all x2, starting transfers between devices, exchange(): return lax.all_to_all(blocks.reshape(PEERS, CAP, width), RD, 0, 0)  12.4 us
    pallas_call x1, Pallas kernels, panel_math(): pl.pallas_call(panel_math_kernel, in_specs=[SMEM] * 2 + [VMEM] * 3 + [ANY...  8.85 us
    ppermute x6, starting transfers between devices, shift(): lax.ppermute(x, 'col', [(c, (c // 2 + by) % 4 * 2 + c % 2) for c in range...  8.53 us
    all_to_all x2, waiting for transfers between devices, exchange(): return lax.all_to_all(blocks.reshape(PEERS, CAP, width), RD, 0, 0)  6.01 us
    pallas_call x1, Pallas kernels, fold(): pl.pallas_call(fold_kernel, in_specs=[VMEM] * 2, out_specs=[VMEM] * 2, ou...  5.77 us
    ppermute x6, starting transfers between devices, partner(): return lax.ppermute(x, 'col', [(c, c ^ 1) for c in range(8)])  5.66 us
  transfers between devices with their start and end apart: 14, of which 4 were waited for; matrix products, arithmetic and copies ran while one was open for 1% of the time, Pallas kernels for 22%

profile of v1, /device:TPU:5, one launch (start us, length us, event | category | flops | bytes accessed | tf_op | source)
XLA Modules:
  0.0 108.0 jit_solution(9777863932717176056)
XLA Ops:
  0.7 0.6 pad_add_fusion.where_ref
  1.3 4.4 %make_plan.1 = (s32[8,512]{1,0:T(8,128)S(1)}, s32[1,1536]{1,0:T(1,128)S(1)}, s32[1]{0:T(128)}, f32[1536,128]{1,0:T(8,128)}) custom-call(s32[4]{0:T(128)} %pad_add_fusion.where_ref, s32[1,512]{1,0:T(1,128)} %bitcast.28, s32[1,512]{1,0:T(1,128)} %bitcast.29, f32[128,512]{1,0:T(8,128)} %bitcast.22), custom_call_target="tpu_custom_call" | custom-call | tf_op jit(solution)/shard_map/make_plan/pallas_call | solution.py:162
  5.7 6.9 %all-to-all-start = ((f32[16,96,128]{2,1,0:T(8,128)}), f32[16,96,128]{2,1,0:T(8,128)S(1)}, u32[]{:S(2)}, u32[]{:S(2)}) async-start(f32[16,96,128]{2,1,0:T(8,128)} %bitcast.27), calls=%async_computation | async-start | bytes 1572864 | tf_op jit(solution)/shard_map/all_to_all | solution.py:419
  12.6 1.2 %collective-permute-start.2 = (f32[128,512]{1,0:T(8,128)}, f32[128,512]{1,0:T(8,128)}, u32[]{:S(2)}, u32[]{:S(2)}) collective-permute-start(f32[128,512]{1,0:T(8,128)} %bitcast.23), channel_id=1, source_target_pairs={{0,4},{4,0},{8,12},{12,8},{16,20},{20,16},{24,28},{28,24},{1,5},{5... | collective-permute-start | bytes 786440 | tf_op jit(solution)/shard_map/ppermute | solution.py:564
  13.9 5.0 %pack_rows.1 = f32[1536,512]{1,0:T(8,128)} custom-call(s32[8,512]{1,0:T(8,128)S(1)} %get-tuple-element.808.codes_ref, f32[512,512]{1,0:T(8,128)} %rows_ref.3), custom_call_target="tpu_custom_call" | custom-call | tf_op jit(solution)/shard_map/pack_rows/pallas_call | solution.py:190
  18.8 6.0 %all-to-all-done.got_ref = f32[16,96,128]{2,1,0:T(8,128)S(1)} async-done(((f32[16,96,128]{2,1,0:T(8,128)}), f32[16,96,128]{2,1,0:T(8,128)S(1)}, u32[]{:S(2)}, u32[]{:S(2)}) %all-to-all-start) | async-done | bytes 786464 | tf_op jit(solution)/shard_map/all_to_all | solution.py:419
  24.8 5.5 %all-to-all-start.1 = ((f32[16,96,512]{2,1,0:T(8,128)}), f32[16,96,512]{2,1,0:T(8,128)}, u32[]{:S(2)}, u32[]{:S(2)}) async-start(f32[16,96,512]{2,1,0:T(8,128)} %bitcast.26), calls=%async_computation.1 | async-start | bytes 6291456 | tf_op jit(solution)/shard_map/all_to_all | solution.py:419
  30.3 0.0 copy-done.6
  30.3 0.0 copy-done.8
  30.3 0.0 copy-start.4
  30.3 0.6 while.66
  31.0 0.0 copy-done.4
  31.0 2.3 %panel_rows.1 = (f32[352,128]{1,0:T(8,128)S(1)}, f32[352,128]{1,0:T(8,128)S(1)}, f32[512,128]{1,0:T(8,128)S(1)}) custom-call(s32[4]{0:T(128)S(1)} %copy-done.4, s32[1]{0:T(128)} %get-tuple-element.525.flag_ref, s32[1,1536]{1,0:T(1,128)S(1)} %get-tuple-element.940, f32[16,96,128]{2,1,0:T(8,128)S(1)} %all-to-all-done.got_ref, f32[1536,640]{1,0:T(8,128)} %get-tuple-element.931), custom_call_target="tpu_custom_call" | custom-call | tf_op jit(solution)/shard_map/panel_rows/pallas_call | solution.py:250
  33.3 0.0 copy-start.2
  33.3 2.6 %collective-permute-start.6 = (f32[352,128]{1,0:T(8,128)S(1)}, f32[352,128]{1,0:T(8,128)S(1)}, u32[]{:S(2)}, u32[]{:S(2)}) collective-permute-start(f32[352,128]{1,0:T(8,128)S(1)} %get-tuple-element.536), channel_id=1, source_target_pairs={{0,4},{4,0},{8,12},{12,8},{16,20},{20,16},{24,28},{28,24},{1,5},{5... | collective-permute-start | bytes 540680 | tf_op jit(solution)/shard_map/ppermute | solution.py:564
  35.9 0.0 collective-permute-done.2
  35.9 1.0 pad_maximum_fusion.p0
  36.9 0.0 collective-permute-done.6
  37.0 0.0 copy-start.1
  37.0 1.7 %collective-permute-start.7 = (f32[704,128]{1,0:T(8,128)S(1)}, f32[704,128]{1,0:T(8,128)}, u32[]{:S(2)}, u32[]{:S(2)}) collective-permute-start(f32[704,128]{1,0:T(8,128)S(1)} %constant_dynamic-update-slice_fusion.k0), channel_id=1, source_target_pairs={{0,8},{4,12},{8,16},{12,20},{16,24},{20,28},{24,0},{28,4},{1,9},{5... | collective-permute-start | bytes 1081352 | tf_op jit(solution)/shard_map/ppermute | solution.py:568
  38.7 1.6 %collective-permute-start.3 = (f32[256,512]{1,0:T(8,128)S(1)}, f32[256,512]{1,0:T(8,128)S(1)}, u32[]{:S(2)}, u32[]{:S(2)}) collective-permute-start(f32[256,512]{1,0:T(8,128)S(1)} %pad_maximum_fusion.p0), channel_id=1, source_target_pairs={{0,8},{4,12},{8,16},{12,20},{16,24},{20,28},{24,0},{28,4},{1,9},{5... | collective-permute-start | bytes 1572872 | tf_op jit(solution)/shard_map/ppermute | solution.py:568
  40.3 1.7 %collective-permute-start.4 = (f32[256,512]{1,0:T(8,128)S(1)}, f32[256,512]{1,0:T(8,128)}, u32[]{:S(2)}, u32[]{:S(2)}) collective-permute-start(f32[256,512]{1,0:T(8,128)S(1)} %pad_maximum_fusion.p0), channel_id=1, source_target_pairs={{0,16},{4,20},{8,24},{12,28},{16,0},{20,4},{24,8},{28,12},{1,17},{... | collective-permute-start | bytes 1572872 | tf_op jit(solution)/shard_map/ppermute | solution.py:568
  42.1 1.2 %collective-permute-start.8 = (f32[704,128]{1,0:T(8,128)S(1)}, f32[704,128]{1,0:T(8,128)}, u32[]{:S(2)}, u32[]{:S(2)}) collective-permute-start(f32[704,128]{1,0:T(8,128)S(1)} %constant_dynamic-update-slice_fusion.k0), channel_id=1, source_target_pairs={{0,16},{4,20},{8,24},{12,28},{16,0},{20,4},{24,8},{28,12},{1,17},{... | collective-permute-start | bytes 1081352 | tf_op jit(solution)/shard_map/ppermute | solution.py:568
  43.3 1.0 collective-permute-start.9
  44.3 5.0 %collective-permute-done.7.k1 = f32[704,128]{1,0:T(8,128)} collective-permute-done((f32[704,128]{1,0:T(8,128)S(1)}, f32[704,128]{1,0:T(8,128)}, u32[]{:S(2)}, u32[]{:S(2)}) %collective-permute-start.7) | collective-permute-done | bytes 360480 | tf_op jit(solution)/shard_map/ppermute | solution.py:568
  49.3 0.0 copy-done.2
  49.3 1.2 %collective-permute-start.5 = (f32[256,512]{1,0:T(8,128)S(1)}, f32[256,512]{1,0:T(8,128)}, u32[]{:S(2)}, u32[]{:S(2)}) collective-permute-start(f32[256,512]{1,0:T(8,128)S(1)} %pad_maximum_fusion.p0), channel_id=1, source_target_pairs={{0,24},{4,28},{8,0},{12,4},{16,8},{20,12},{24,16},{28,20},{1,25},{... | collective-permute-start | bytes 1572872 | tf_op jit(solution)/shard_map/ppermute | solution.py:568
  50.5 5.8 %fold_slots.1 = (bf16[2,512,1024]{2,1,0:T(8,128)(2,1)}, bf16[2,512,1024]{2,1,0:T(8,128)(2,1)}) custom-call(s32[1,1536]{1,0:T(1,128)S(1)} %get-tuple-element.940, f32[2,512,512]{2,1,0:T(8,128)} %get-tuple-element.942), custom_call_target="tpu_custom_call" | custom-call | tf_op jit(solution)/shard_map/fold_slots/pallas_call | solution.py:271
  56.3 24.1 %collective-permute-done.8.k2 = f32[704,128]{1,0:T(8,128)} collective-permute-done((f32[704,128]{1,0:T(8,128)S(1)}, f32[704,128]{1,0:T(8,128)}, u32[]{:S(2)}, u32[]{:S(2)}) %collective-permute-start.8) | collective-permute-done | bytes 360480 | tf_op jit(solution)/shard_map/ppermute | solution.py:568
  80.4 1.2 %collective-permute-start.10 = (f32[704,128]{1,0:T(8,128)S(1)}, f32[704,128]{1,0:T(8,128)S(1)}, u32[]{:S(2)}, u32[]{:S(2)}) collective-permute-start(f32[704,128]{1,0:T(8,128)S(1)} %constant_dynamic-update-slice_fusion.k0), channel_id=1, source_target_pairs={{0,4},{4,0},{8,12},{12,8},{16,20},{20,16},{24,28},{28,24},{1,5},{5... | collective-permute-start | bytes 1081352 | tf_op jit(solution)/shard_map/ppermute | solution.py:564
  81.6 0.0 collective-permute-done.9.k3
  81.7 0.0 collective-permute-start.11
  81.7 0.0 collective-permute-done.3.p1
  81.7 0.5 collective-permute-start.12
  82.2 0.0 collective-permute-done.4.p2
  82.2 0.1 collective-permute-start.13
  82.3 0.0 collective-permute-done.5.p3
  82.3 1.9 %own_panels.1.whole_ref = f32[2,512,512]{2,1,0:T(8,128)S(1)} custom-call(s32[4]{0:T(128)S(1)} %copy-done.4, f32[256,512]{1,0:T(8,128)S(1)} %pad_maximum_fusion.p0, f32[256,512]{1,0:T(8,128)S(1)} %collective-permute-done.3.p1, f32[256,512]{1,0:T(8,128)} %collective-permute-done.4.p2, f32[256,512]{1,0:T(8,128)} %collective-permute-done.5.p3), custom_call_target="tpu_custom_call" | custom-call | tf_op jit(solution)/shard_map/own_panels/pallas_call | solution.py:288
  84.2 0.0 collective-permute-done.10.p0
  84.2 0.0 collective-permute-done.11.p1
  84.2 0.0 collective-permute-done.12.p2
  84.2 0.3 collective-permute-done.13.p3
  84.6 0.0 copy-done.1
  84.6 0.0 copy-done.3
  84.6 8.8 %panel_math.1 = (bf16[6,512,512]{2,1,0:T(8,128)(2,1)S(1)}, f32[128,512]{1,0:T(8,128)}) custom-call(s32[4]{0:T(128)S(1)} %copy-done.4, s32[1]{0:T(128)} %get-tuple-element.525.flag_ref, s32[1,1536]{1,0:T(1,128)S(1)} %get-tuple-element.940, f32[512,128]{1,0:T(8,128)S(1)} %copy-done.3, f32[2,512,512]{2,1,0:T(8,128)S(1)} %own_panels.1.whole_ref, ...), custom_call_target="tpu_custom_call" | custom-call | tf_op jit(solution)/shard_map/panel_math/pallas_call | solution.py:349
  93.4 1.6 %copy-done = bf16[6,512,512]{2,1,0:T(8,128)(2,1)} copy-done((bf16[6,512,512]{2,1,0:T(8,128)(2,1)}, bf16[6,512,512]{2,1,0:T(8,128)(2,1)S(1)}, u32[]{:S(2)}) %copy-start) | copy-done | bytes 3145752
  95.1 0.0 all-to-all-done.1.got_ref
  95.1 12.8 %slab_math.1 = f32[512,512]{1,0:T(8,128)} custom-call(s32[4]{0:T(128)} %pad_add_fusion.where_ref, s32[1]{0:T(128)} %get-tuple-element.525.flag_ref, s32[1,1536]{1,0:T(1,128)S(1)} %get-tuple-element.940, f32[16,96,512]{2,1,0:T(8,128)} %all-to-all-done.1.got_ref, f32[512,512]{1,0:T(8,128)} %rows_ref.3, f32[1536,512]{1,0:T(8,128)} %get-tuple-element.933, ...), custom_call_target="tpu_custom_call" | custom-call | tf_op jit(solution)/shard_map/slab_math/pallas_call | solution.py:396
  (9 shorter events, 0.0 us)
Async XLA Ops:
  5.7 19.1 %all-to-all-start = ((f32[16,96,128]{2,1,0:T(8,128)}), f32[16,96,128]{2,1,0:T(8,128)S(1)}, u32[]{:S(2)}, u32[]{:S(2)}) async-start(f32[16,96,128]{2,1,0:T(8,128)} %bitcast.27), calls=%async_computation | async-start | bytes 1572864 | tf_op jit(solution)/shard_map/all_to_all | solution.py:419
  12.6 23.3 %collective-permute-start.2 = (f32[128,512]{1,0:T(8,128)}, f32[128,512]{1,0:T(8,128)}, u32[]{:S(2)}, u32[]{:S(2)}) collective-permute-start(f32[128,512]{1,0:T(8,128)} %bitcast.23), channel_id=1, source_target_pairs={{0,4},{4,0},{8,12},{12,8},{16,20},{20,16},{24,28},{28,24},{1,5},{5... | collective-permute-start | bytes 786440 | tf_op jit(solution)/shard_map/ppermute | solution.py:564
  24.8 5.5 %copy-start.6 = (f32[512,512]{1,0:T(8,128)S(1)}, f32[512,512]{1,0:T(8,128)}, u32[]{:S(2)}) copy-start(f32[512,512]{1,0:T(8,128)} %rows_ref.3) | copy-start | bytes 3145732
  24.8 5.5 %copy-start.8 = (f32[2,512,64]{1,2,0:T(8,128)S(1)}, f32[2,512,64]{1,2,0:T(8,128)}, u32[]{:S(2)}) copy-start(f32[2,512,64]{1,2,0:T(8,128)} %param.12) | copy-start | bytes 786436
  24.8 70.2 %all-to-all-start.1 = ((f32[16,96,512]{2,1,0:T(8,128)}), f32[16,96,512]{2,1,0:T(8,128)}, u32[]{:S(2)}, u32[]{:S(2)}) async-start(f32[16,96,512]{2,1,0:T(8,128)} %bitcast.26), calls=%async_computation.1 | async-start | bytes 6291456 | tf_op jit(solution)/shard_map/all_to_all | solution.py:419
  30.3 0.7 copy-start.4
  33.3 16.0 %copy-start.2 = (f32[512,128]{1,0:T(8,128)}, f32[512,128]{1,0:T(8,128)S(1)}, u32[]{:S(2)}) copy-start(f32[512,128]{1,0:T(8,128)S(1)} %get-tuple-element.533.tops_ref) | copy-start | bytes 786436
  33.3 3.6 %collective-permute-start.6 = (f32[352,128]{1,0:T(8,128)S(1)}, f32[352,128]{1,0:T(8,128)S(1)}, u32[]{:S(2)}, u32[]{:S(2)}) collective-permute-start(f32[352,128]{1,0:T(8,128)S(1)} %get-tuple-element.536), channel_id=1, source_target_pairs={{0,4},{4,0},{8,12},{12,8},{16,20},{20,16},{24,28},{28,24},{1,5},{5... | collective-permute-start | bytes 540680 | tf_op jit(solution)/shard_map/ppermute | solution.py:564
  37.0 47.6 %copy-start.1 = (f32[2,512,512]{2,1,0:T(8,128)S(1)}, f32[2,512,512]{2,1,0:T(8,128)}, u32[]{:S(2)}) copy-start(f32[2,512,512]{2,1,0:T(8,128)} %upper_ref.1) | copy-start | bytes 6291460
  37.0 12.3 %collective-permute-start.7 = (f32[704,128]{1,0:T(8,128)S(1)}, f32[704,128]{1,0:T(8,128)}, u32[]{:S(2)}, u32[]{:S(2)}) collective-permute-start(f32[704,128]{1,0:T(8,128)S(1)} %constant_dynamic-update-slice_fusion.k0), channel_id=1, source_target_pairs={{0,8},{4,12},{8,16},{12,20},{16,24},{20,28},{24,0},{28,4},{1,9},{5... | collective-permute-start | bytes 1081352 | tf_op jit(solution)/shard_map/ppermute | solution.py:568
  38.7 43.0 %collective-permute-start.3 = (f32[256,512]{1,0:T(8,128)S(1)}, f32[256,512]{1,0:T(8,128)S(1)}, u32[]{:S(2)}, u32[]{:S(2)}) collective-permute-start(f32[256,512]{1,0:T(8,128)S(1)} %pad_maximum_fusion.p0), channel_id=1, source_target_pairs={{0,8},{4,12},{8,16},{12,20},{16,24},{20,28},{24,0},{28,4},{1,9},{5... | collective-permute-start | bytes 1572872 | tf_op jit(solution)/shard_map/ppermute | solution.py:568
  40.3 41.8 %collective-permute-start.4 = (f32[256,512]{1,0:T(8,128)S(1)}, f32[256,512]{1,0:T(8,128)}, u32[]{:S(2)}, u32[]{:S(2)}) collective-permute-start(f32[256,512]{1,0:T(8,128)S(1)} %pad_maximum_fusion.p0), channel_id=1, source_target_pairs={{0,16},{4,20},{8,24},{12,28},{16,0},{20,4},{24,8},{28,12},{1,17},{... | collective-permute-start | bytes 1572872 | tf_op jit(solution)/shard_map/ppermute | solution.py:568
  42.1 38.3 %collective-permute-start.8 = (f32[704,128]{1,0:T(8,128)S(1)}, f32[704,128]{1,0:T(8,128)}, u32[]{:S(2)}, u32[]{:S(2)}) collective-permute-start(f32[704,128]{1,0:T(8,128)S(1)} %constant_dynamic-update-slice_fusion.k0), channel_id=1, source_target_pairs={{0,16},{4,20},{8,24},{12,28},{16,0},{20,4},{24,8},{28,12},{1,17},{... | collective-permute-start | bytes 1081352 | tf_op jit(solution)/shard_map/ppermute | solution.py:568
  43.3 38.4 %collective-permute-start.9 = (f32[704,128]{1,0:T(8,128)S(1)}, f32[704,128]{1,0:T(8,128)}, u32[]{:S(2)}, u32[]{:S(2)}) collective-permute-start(f32[704,128]{1,0:T(8,128)S(1)} %constant_dynamic-update-slice_fusion.k0), channel_id=1, source_target_pairs={{0,24},{4,28},{8,0},{12,4},{16,8},{20,12},{24,16},{28,20},{1,25},{... | collective-permute-start | bytes 1081352 | tf_op jit(solution)/shard_map/ppermute | solution.py:568
  49.3 32.9 %collective-permute-start.5 = (f32[256,512]{1,0:T(8,128)S(1)}, f32[256,512]{1,0:T(8,128)}, u32[]{:S(2)}, u32[]{:S(2)}) collective-permute-start(f32[256,512]{1,0:T(8,128)S(1)} %pad_maximum_fusion.p0), channel_id=1, source_target_pairs={{0,24},{4,28},{8,0},{12,4},{16,8},{20,12},{24,16},{28,20},{1,25},{... | collective-permute-start | bytes 1572872 | tf_op jit(solution)/shard_map/ppermute | solution.py:568
  56.3 28.3 %copy-start.3 = (f32[512,128]{1,0:T(8,128)S(1)}, f32[512,128]{1,0:T(8,128)}, u32[]{:S(2)}) copy-start(f32[512,128]{1,0:T(8,128)} %copy-done.2) | copy-start | bytes 786436
  56.3 28.3 %copy-start.5 = (f32[2,512,512]{2,1,0:T(8,128)S(1)}, f32[2,512,512]{2,1,0:T(8,128)}, u32[]{:S(2)}) copy-start(f32[2,512,512]{2,1,0:T(8,128)} %get-tuple-element.942) | copy-start | bytes 6291460
  80.4 3.8 %collective-permute-start.10 = (f32[704,128]{1,0:T(8,128)S(1)}, f32[704,128]{1,0:T(8,128)S(1)}, u32[]{:S(2)}, u32[]{:S(2)}) collective-permute-start(f32[704,128]{1,0:T(8,128)S(1)} %constant_dynamic-update-slice_fusion.k0), channel_id=1, source_target_pairs={{0,4},{4,0},{8,12},{12,8},{16,20},{20,16},{24,28},{28,24},{1,5},{5... | collective-permute-start | bytes 1081352 | tf_op jit(solution)/shard_map/ppermute | solution.py:564
  81.7 2.6 %collective-permute-start.11 = (f32[704,128]{1,0:T(8,128)}, f32[704,128]{1,0:T(8,128)S(1)}, u32[]{:S(2)}, u32[]{:S(2)}) collective-permute-start(f32[704,128]{1,0:T(8,128)} %collective-permute-done.7.k1), channel_id=1, source_target_pairs={{0,4},{4,0},{8,12},{12,8},{16,20},{20,16},{24,28},{28,24},{1,5},{5... | collective-permute-start | bytes 1081352 | tf_op jit(solution)/shard_map/ppermute | solution.py:564
  81.7 2.6 %collective-permute-start.12 = (f32[704,128]{1,0:T(8,128)}, f32[704,128]{1,0:T(8,128)S(1)}, u32[]{:S(2)}, u32[]{:S(2)}) collective-permute-start(f32[704,128]{1,0:T(8,128)} %collective-permute-done.8.k2), channel_id=1, source_target_pairs={{0,4},{4,0},{8,12},{12,8},{16,20},{20,16},{24,28},{28,24},{1,5},{5... | collective-permute-start | bytes 1081352 | tf_op jit(solution)/shard_map/ppermute | solution.py:564
  82.2 2.4 %collective-permute-start.13 = (f32[704,128]{1,0:T(8,128)}, f32[704,128]{1,0:T(8,128)S(1)}, u32[]{:S(2)}, u32[]{:S(2)}) collective-permute-start(f32[704,128]{1,0:T(8,128)} %collective-permute-done.9.k3), channel_id=1, source_target_pairs={{0,4},{4,0},{8,12},{12,8},{16,20},{20,16},{24,28},{28,24},{1,5},{5... | collective-permute-start | bytes 1081352 | tf_op jit(solution)/shard_map/ppermute | solution.py:564
  93.4 1.6 %copy-start = (bf16[6,512,512]{2,1,0:T(8,128)(2,1)}, bf16[6,512,512]{2,1,0:T(8,128)(2,1)S(1)}, u32[]{:S(2)}) copy-start(bf16[6,512,512]{2,1,0:T(8,128)(2,1)S(1)} %get-tuple-element.546.left_ref) | copy-start | bytes 9437188
